TPU v7x, 256 devices: a whole 4x4x8 slice. The times are simulated.
256 devices in a mesh: sta: 64 (over x, z, core), seg: 4 (over y).
Axes of the slice: x: 4, y: 4, z: 8, core: 2. Of those that a mesh axis runs over, the one named last changes fastest.
Arguments:
- traces: float32 [1024, 8, 4096], P('sta', 'seg'), may hold values from -60 to 60, as said below
- pair_blocks: int32 [2048, 2], P('sta'), may hold values from 0 to 255, as said below
- pair_counts: int32 [64], P('sta'), may hold values from 4 to 32, as said below
Outputs:
- correlations: bfloat16 [2048, 4, 4, 4096], P(('sta', 'seg'))
Inputs may be any that keep to these rules, and one draw needn't show every extreme that they name: `traces`: random scales per station. `pair_blocks`: rows k * 32 to (k + 1) * 32 - 1 belong to owner k: their first block is one of owner k's stations' blocks, numbers k * 4 to (k + 1) * 4 - 1. Over the 32 rows of one owner, at most 1 second blocks lie in the blocks of any one index of sta, and every owner has exactly 1 for some index. `pair_counts`: one owner has exactly 32 live slots; live slots are the first ones of an owner.
All inputs are finite; a program needn't handle non-finite values.
Results may differ from a plain program's by a relative error of at most 0.0057.
Values may be sent and summed in bfloat16 or wider, within the bound.
A program may use at most 128 MiB of HBM per device.

v0:
```python
import functools
import math

import jax
import jax.numpy as jnp
import ml_dtypes
import numpy as np
from jax import lax
from jax.experimental import pallas as pl
from jax.experimental.pallas import tpu as pltpu
from jax.sharding import PartitionSpec as P

MESH = pl.DeviceIdType.MESH
F32 = jnp.float32
BF16 = jnp.bfloat16
HIGHEST = lax.Precision.HIGHEST
EPSILON = 1e-06
NX, NZ, NY = 4, 8, 4
CHUNKS = 4
SLOTS = 32
MIB = 1 << 20


def split_high(table):
    high = table.astype(ml_dtypes.bfloat16)
    return high, (table - high.astype(np.float64)).astype(ml_dtypes.bfloat16)


def forward_tables():
    a = np.arange(32)
    outer = np.zeros((2, 16, 2, 4, 2, 4, 32, 2))
    for c in range(16):
        for e in range(2):
            angle = 2 * np.pi * (a * (2 * c + e) % 32) / 32
            for g in range(2):
                for j in range(4):
                    outer[0, c, g, j, e, j, :, g] = np.cos(angle)
                    outer[1, c, g, j, e, j, :, g] = -np.sin(angle)
    k = np.broadcast_to(2 * np.arange(16)[:, None, None] + np.arange(2), (16, 8, 2)).reshape(256)
    twist = 2 * np.pi * (k[:, None] * np.arange(128)) / 4096
    inner = 2 * np.pi * (np.arange(128)[:, None] * np.arange(64) % 128) / 128
    cos, sin = np.cos(inner), np.sin(inner)
    inner = np.concatenate([np.concatenate([cos, -sin], 1), np.concatenate([sin, cos], 1)], 0)
    return tuple(
        t.astype(np.float32) for t in (outer.reshape(512, 256), np.cos(twist), np.sin(twist), inner)
    )


def inverse_tables():
    inner = 2 * np.pi * (np.arange(64)[:, None] * np.arange(128) % 128) / 128
    cos, sin = np.cos(inner) / 64, np.sin(inner) / 64
    inner = np.concatenate([np.concatenate([cos, sin], 1), np.concatenate([-sin, cos], 1)], 0)
    inner = np.concatenate(split_high(inner), 0)
    k = np.broadcast_to(2 * np.arange(16)[:, None, None] + np.arange(2), (16, 4, 2)).reshape(16, 8)
    twist = 2 * np.pi * (k[:, :, None] * np.arange(128)) / 4096
    outer = np.zeros((32, 4, 2, 16, 4, 2))
    u = np.arange(32)
    for c in range(16):
        for e in range(2):
            angle = 2 * np.pi * (u * (2 * c + e) % 32) / 32
            for j in range(4):
                outer[:, j, 0, c, j, e] = np.cos(angle)
                outer[:, j, 1, c, j, e] = -np.sin(angle)
    high, low = split_high(outer.reshape(128, 256))
    outer = np.concatenate([high, high, low], 1)
    weight = np.ones((32, 128))
    weight[::2, 0] = 0.5
    return (
        inner,
        np.cos(twist).astype(np.float32),
        np.sin(twist).astype(np.float32),
        outer,
        weight.astype(ml_dtypes.bfloat16),
    )


def whiten_kernel(x_ref, pairs_ref, outer_ref, cos_ref, sin_ref, inner_ref, white_ref, need_ref):
    x = x_ref[...].reshape(16, 8, 8, 128)
    total = jnp.sum(x, axis=1)
    total = total + pltpu.roll(total, 4, 1)
    total = total + pltpu.roll(total, 2, 1)
    mean = jnp.sum(total, axis=-1, keepdims=True) * (1.0 / 4096)
    x = (x - mean[:, None]).reshape(4, 256, 128)
    row = lax.broadcasted_iota(jnp.int32, (2, 8, 128), 1)
    lane = lax.broadcasted_iota(jnp.int32, (2, 8, 128), 2)
    cos, sin = cos_ref[...], sin_ref[...]
    for half in range(2):
        both = jnp.concatenate([x[2 * half], x[2 * half + 1]], axis=1)
        section = jnp.dot(outer_ref[...], both, precision=HIGHEST, preferred_element_type=F32)
        for b in range(2):
            real = section[:256, 128 * b : 128 * b + 128]
            imag = section[256:, 128 * b : 128 * b + 128]
            turned = jnp.concatenate([real * cos + imag * sin, imag * cos - real * sin], axis=1)
            spec = jnp.dot(turned, inner_ref[...], precision=HIGHEST, preferred_element_type=F32)
            spec = spec.reshape(16, 2, 8, 128)
            power = jnp.sum(spec * spec, axis=0)
            power = power + jnp.where(row % 2 == 0, pltpu.roll(power, 7, 1), pltpu.roll(power, 1, 1))
            power = power + jnp.where(lane % 2 == 0, pltpu.roll(power, 127, 2), pltpu.roll(power, 1, 2))
            power = power + pltpu.roll(power, 64, 2)
            white = spec * (1.0 / jnp.sqrt(power * (1.0 / 64) + EPSILON))
            white_ref[:, :, 2 * half + b] = white.reshape(4, 4, 16, 128).astype(BF16)
    partner = pairs_ref[:, 1:2]
    source = lax.broadcasted_iota(jnp.int32, (SLOTS, 128), 1)
    need = jnp.sum(jnp.where(partner // 4 == source, partner % 4, 0), axis=0, keepdims=True)
    need_ref[...] = jnp.broadcast_to(need, (8, 128))


def exchange_kernel(
    white_ref,
    need_ref,
    pairs_ref,
    stacked_ref,
    *scratch,
):
    ring, chosen = scratch[:CHUNKS], scratch[CHUNKS : 2 * CHUNKS]
    picked, sides, cross, table, lookup, need_sem, table_sem, own_sem, y_sem, z_sem, x_sem, c_sem, keep_sem = scratch[
        2 * CHUNKS :
    ]
    sta, q = lax.axis_index("sta"), lax.axis_index("seg")
    x, z, core = sta // 16, sta // 2 % 8, sta % 2

    def at(dx, dz, flip):
        other = core if flip == 0 else 1 - core
        return (((x + dx) % NX * NZ + (z + dz) % NZ) * 2 + other, q)

    def along(dy):
        return (sta, (q + dy) % NY)

    row_peers = [(d, f) for d in range(NX) for f in range(2) if (d, f) != (0, 0)]
    targets = [along(r) for r in range(1, NY)] + [at(0, 1, 0), at(0, NZ - 1, 0)]
    targets += [at(d, 0, f) for d, f in row_peers]
    barrier = pltpu.get_barrier_semaphore()
    for target in targets:
        pl.semaphore_signal(barrier, inc=1, device_id=target, device_id_type=MESH)
    pl.semaphore_wait(barrier, len(targets))

    started = []

    def send(source, destination, sems, target):
        copy = pltpu.make_async_remote_copy(
            source, destination, sems.at[0], sems.at[1], device_id=target, device_id_type=MESH
        )
        copy.start()
        started.append(copy)
        return copy

    own = []
    y_in = [[] for _ in range(CHUNKS)]
    for c in range(CHUNKS):
        for r in range(1, NY):
            y_in[c].append(
                send(white_ref.at[(q + r) % NY, c], ring[c].at[0, r], y_sem.at[c, r], along(r))
            )
        copy = pltpu.make_async_copy(white_ref.at[q, c], ring[c].at[0, 0], own_sem.at[c])
        copy.start()
        own.append(copy)
    need_in = [
        send(need_ref, table.at[d * 2 + f], need_sem.at[d * 2 + f], at(d, 0, f)) for d, f in row_peers
    ]
    table[0] = need_ref[...]

    def gather_ring(c):
        own[c].wait()
        for copy in y_in[c]:
            copy.wait_recv()
        for t in range(1, 5):
            copies = []
            if t < 4 or c % 2 == 0:
                copies.append(send(ring[c].at[t - 1], ring[c].at[t], z_sem.at[c, t], at(0, 1, 0)))
            if t < 4 or c % 2 == 1:
                copies.append(
                    send(ring[c].at[(9 - t) % 8], ring[c].at[8 - t], z_sem.at[c, 8 - t], at(0, NZ - 1, 0))
                )
            for copy in copies:
                copy.wait_recv()

    def pick(c):
        def one(slot, carry):
            for dz in range(NZ):
                block = lookup[slot, 0, (x * NZ + (z - dz) % NZ) * 2 + core]
                picked[c, slot, dz] = ring[c][dz, :, block]
            return carry

        lax.fori_loop(0, 2 * NX, one, 0)
        chosen[c][0] = picked[c, 0]

    def spread(c):
        return [
            send(picked.at[c, d * 2 + f], chosen[c].at[(NX - d) % NX * 2 + f], x_sem.at[c, d * 2 + f], at(-d, 0, f))
            for d, f in row_peers
        ]

    row = lax.broadcasted_iota(jnp.int32, (8, 128), 0)
    left = lax.broadcasted_iota(jnp.int32, (8, 128), 1) < 64

    def prepare(c):
        def one(step, carry):
            b, r = step // NY, step % NY
            both = ring[c][0, r, b].astype(F32)
            for g in range(2):
                value = both[8 * g : 8 * g + 8]
                turned = pltpu.roll(value, 64, 1)
                for part, side in enumerate(
                    (jnp.where(left, value, -turned), jnp.where(left, turned, value))
                ):
                    for i in range(4):
                        only = jnp.where(row // 2 == i, side, 0.0)
                        only = only + pltpu.roll(only, 2, 0)
                        sides[b, part, i, r * 2 + g] = only + pltpu.roll(only, 4, 0)
            return carry

        lax.fori_loop(0, 4 * NY, one, 0)

    def multiply(c):
        def one(slot, carry):
            first = pairs_ref[slot, 0] % 4
            partner = pairs_ref[slot, 1] // 4
            dx, dz, flip = (x - partner // 16) % NX, (z - partner // 2 % 8) % NZ, (core + partner) % 2
            second = chosen[c][dx * 2 + flip, dz].astype(F32)
            rows = []
            for i in range(4):
                straight = sides[first, 0, i, 0] * second[0, 0:8]
                crossed = sides[first, 1, i, 0] * second[0, 0:8]
                for g in range(1, 8):
                    part = second[g // 2, 8 * (g % 2) : 8 * (g % 2) + 8]
                    straight = straight + sides[first, 0, i, g] * part
                    crossed = crossed + sides[first, 1, i, g] * part
                rows.append(straight + pltpu.roll(crossed, 64, 1))
            cross[c, slot] = jnp.concatenate(rows, axis=0).astype(BF16)
            return carry

        lax.fori_loop(0, SLOTS, one, 0)

    last = []

    def hand_over(c):
        for r in range(1, NY):
            last.append(
                send(
                    cross.at[c, pl.ds((q + r) % NY * 8, 8)],
                    stacked_ref.at[q, c],
                    c_sem.at[c, r],
                    along(r),
                )
            )
        copy = pltpu.make_async_copy(cross.at[c, pl.ds(q * 8, 8)], stacked_ref.at[q, c], keep_sem.at[c])
        copy.start()
        return copy

    kept = []
    x_in = {}

    def finish(c):
        prepare(c)
        for copy in x_in[c]:
            copy.wait_recv()
        multiply(c)
        kept.append(hand_over(c))

    gather_ring(0)
    for copy in need_in:
        copy.wait_recv()
    copy = pltpu.make_async_copy(table, lookup, table_sem)
    copy.start()
    copy.wait()
    for c in range(CHUNKS):
        if c:
            gather_ring(c)
        pick(c)
        x_in[c] = spread(c)
        if c:
            finish(c - 1)
    finish(CHUNKS - 1)
    for copy in kept:
        copy.wait()
    for copy in last:
        copy.wait_recv()
    for copy in started:
        copy.wait_send()


def invert_kernel(counts_ref, stacked_ref, inner_ref, cos_ref, sin_ref, outer_ref, weight_ref, out_ref):
    slot = lax.axis_index("seg") * 8 + pl.program_id(0)
    live = (slot < counts_ref[0]).astype(F32)
    cross = stacked_ref[:, :, 0].reshape(16, 32, 128)
    cross = jnp.concatenate([cross[0:1] * weight_ref[...], cross[1:]], axis=0).reshape(512, 128)
    series = jnp.dot(jnp.concatenate([cross, cross], axis=1), inner_ref[...], preferred_element_type=F32)
    series = series.reshape(16, 4, 8, 256)
    cos, sin = cos_ref[...] * live, sin_ref[...] * live
    parts = []
    for i in range(4):
        real, imag = series[:, i, :, :128], series[:, i, :, 128:]
        turned = jnp.concatenate(
            [(real * cos - imag * sin).reshape(128, 128), (real * sin + imag * cos).reshape(128, 128)], axis=0
        )
        parts.append(turned)
    for pair in range(2):
        both = jnp.concatenate([parts[2 * pair], parts[2 * pair + 1]], axis=1)
        high = both.astype(BF16)
        low = (both - high.astype(F32)).astype(BF16)
        lags = jnp.dot(
            outer_ref[...], jnp.concatenate([high, low, high], axis=0), preferred_element_type=F32
        ).astype(BF16)
        out_ref[0, 2 * pair] = lags[:, :128]
        out_ref[0, 2 * pair + 1] = lags[:, 128:]


def vmem():
    return pl.BlockSpec(memory_space=pltpu.VMEM)


def local(traces, pair_blocks, pair_counts):
    stations, segs, length = traces.shape
    rows = traces.reshape(stations, segs, 32, 128).transpose(0, 2, 1, 3).reshape(1024, 128)
    white, need = pl.pallas_call(
        whiten_kernel,
        out_shape=(
            jax.ShapeDtypeStruct((NY, CHUNKS, 4, 16, 128), BF16),
            jax.ShapeDtypeStruct((8, 128), jnp.int32),
        ),
        in_specs=[vmem()] * 6,
        out_specs=(vmem(), vmem()),
        compiler_params=pltpu.CompilerParams(vmem_limit_bytes=32 * MIB),
        name="whiten",
    )(rows, pair_blocks, *forward_tables())
    dma = pltpu.SemaphoreType.DMA
    stacked = pl.pallas_call(
        exchange_kernel,
        out_shape=jax.ShapeDtypeStruct((NY, CHUNKS, 8, 32, 128), BF16),
        in_specs=[vmem(), vmem(), pl.BlockSpec(memory_space=pltpu.SMEM)],
        out_specs=pl.BlockSpec(memory_space=pl.ANY),
        scratch_shapes=[
            *[pltpu.VMEM((NZ, NY, 4, 16, 128), BF16)] * CHUNKS,
            *[pltpu.VMEM((2 * NX, NZ, NY, 16, 128), BF16)] * CHUNKS,
            pltpu.VMEM((CHUNKS, 2 * NX, NZ, NY, 16, 128), BF16),
            pltpu.VMEM((4, 2, 4, 8, 8, 128), F32),
            pltpu.VMEM((CHUNKS, SLOTS, 32, 128), BF16),
            pltpu.VMEM((2 * NX, 8, 128), jnp.int32),
            pltpu.SMEM((2 * NX, 8, 128), jnp.int32),
            dma((2 * NX, 2)),
            dma(()),
            dma((CHUNKS,)),
            dma((CHUNKS, NY, 2)),
            dma((CHUNKS, NZ, 2)),
            dma((CHUNKS, 2 * NX, 2)),
            dma((CHUNKS, NY, 2)),
            dma((CHUNKS,)),
        ],
        compiler_params=pltpu.CompilerParams(
            collective_id=0, has_side_effects=True, vmem_limit_bytes=40 * MIB
        ),
        name="exchange",
    )(white, need, pair_blocks)
    whole = lambda *shape: pl.BlockSpec(shape, lambda p: (0,) * len(shape))
    lags = pl.pallas_call(
        invert_kernel,
        out_shape=jax.ShapeDtypeStruct((8, 4, 128, 128), BF16),
        grid=(8,),
        in_specs=[
            pl.BlockSpec(memory_space=pltpu.SMEM),
            pl.BlockSpec((NY, CHUNKS, 1, 32, 128), lambda p: (0, 0, p, 0, 0)),
            whole(256, 256),
            whole(16, 8, 128),
            whole(16, 8, 128),
            whole(128, 768),
            whole(32, 128),
        ],
        out_specs=pl.BlockSpec((1, 4, 128, 128), lambda p: (p, 0, 0, 0)),
        compiler_params=pltpu.CompilerParams(vmem_limit_bytes=32 * MIB),
        name="invert",
    )(pair_counts, stacked, *inverse_tables())
    return lags.reshape(8, 4, 32, 4, 128).transpose(0, 1, 3, 2, 4).reshape(8, 4, 4, length)


def solution(mesh):
    in_specs = (P("sta", "seg", None), P("sta", None), P("sta"))
    out_specs = P(("sta", "seg"), None, None, None)
    return jax.shard_map(local, mesh=mesh, in_specs=in_specs, out_specs=out_specs, check_vma=False)
```

profile of v0, /device:TPU:1, one launch (start us, length us, event | category | flops | bytes accessed | tf_op | source)
XLA Modules:
  0.0 119.1 jit_solution(12932289096516545792)
XLA Ops:
  0.7 0.0 copy-start.10
  0.7 0.7 copy-done.10
  1.3 0.1 copy.14.pairs_ref
  1.4 0.0 copy-start
  1.4 1.0 copy-done
  2.5 0.0 copy-start.1
  2.5 1.0 copy-done.1
  3.5 0.0 copy-start.4
  3.5 0.9 copy-done.4
  4.4 0.0 copy-start.5
  4.4 0.9 copy-done.5
  5.3 0.0 copy-start.6
  5.3 0.9 copy-done.6
  6.2 3.0 %whiten.1 = (bf16[4,4,4,16,128]{4,3,2,1,0:T(8,128)(2,1)S(1)}, s32[8,128]{1,0:T(8,128)S(1)}) custom-call(f32[1024,128]{1,0:T(8,128)S(1)} %bitcast.10, s32[32,2]{1,0:T(8,128)S(1)} %copy.14.pairs_ref, f32[512,256]{1,0:T(8,128)S(1)} %copy-done.1, f32[256,128]{1,0:T(8,128)S(1)} %copy-done.6, f32[256,128]{1,0:T(8,128)S(1)} %copy-done.5, f32[256,128]{1,0:T(8,128)S(1)} %copy-done.4), custom_call_target="tpu_custom_call" | custom-call | tf_op jit(solution)/shard_map/whiten/pallas_call | solution.py:315
  9.2 0.0 copy-start.2
  9.2 0.0 copy-start.3
  9.3 0.0 copy-start.7
  9.3 0.0 copy-start.8
  9.3 0.0 copy-start.9
  9.3 104.0 %exchange.1.stacked_ref = bf16[4,4,8,32,128]{4,3,2,1,0:T(8,128)(2,1)S(1)} custom-call(bf16[4,4,4,16,128]{4,3,2,1,0:T(8,128)(2,1)S(1)} %get-tuple-element.7.white_ref, s32[8,128]{1,0:T(8,128)S(1)} %get-tuple-element.8.need_ref, s32[32,2]{1,0:T(8,128)S(1)} %copy.14.pairs_ref), custom_call_target="tpu_custom_call" | custom-call | tf_op jit(solution)/shard_map/exchange/pallas_call | solution.py:327
  113.3 0.0 copy-done.2
  113.3 0.0 copy-done.3
  113.3 0.0 copy-done.7
  113.4 0.0 copy-done.8
  113.4 0.0 copy-done.9
  113.4 5.7 %invert.1 = bf16[8,4,128,128]{3,2,1,0:T(8,128)(2,1)} custom-call(s32[1]{0:T(128)S(6)} %copy.17.counts_ref, bf16[4,4,8,32,128]{4,3,2,1,0:T(8,128)(2,1)S(1)} %exchange.1.stacked_ref, bf16[256,256]{1,0:T(8,128)(2,1)S(1)} %copy-done.3, f32[16,8,128]{2,1,0:T(8,128)S(1)} %copy-done.8, f32[16,8,128]{2,1,0:T(8,128)S(1)} %copy-done.7, ...), custom_call_target="tpu_custom_call" | custom-call | tf_op jit(solution)/shard_map/invert/pallas_call | solution.py:355
Async XLA Ops:
  0.7 0.7 copy-start.10
  1.4 1.0 copy-start
  2.5 1.0 copy-start.1
  3.5 0.9 copy-start.4
  4.4 0.9 copy-start.5
  5.3 0.9 copy-start.6
  9.2 104.1 %copy-start.2 = (bf16[128,768]{1,0:T(8,128)(2,1)S(1)}, bf16[128,768]{1,0:T(8,128)(2,1)}, u32[]{:S(2)}) copy-start(bf16[128,768]{1,0:T(8,128)(2,1)} %constant.25.clone.outer_ref) | copy-start | bytes 589828
  9.2 104.1 %copy-start.3 = (bf16[256,256]{1,0:T(8,128)(2,1)S(1)}, bf16[256,256]{1,0:T(8,128)(2,1)}, u32[]{:S(2)}) copy-start(bf16[256,256]{1,0:T(8,128)(2,1)} %constant.22.clone.inner_ref) | copy-start | bytes 393220
  9.3 104.1 %copy-start.7 = (f32[16,8,128]{2,1,0:T(8,128)S(1)}, f32[16,8,128]{2,1,0:T(8,128)}, u32[]{:S(2)}) copy-start(f32[16,8,128]{2,1,0:T(8,128)} %constant.24.clone.sin_ref) | copy-start | bytes 196612
  9.3 104.1 %copy-start.8 = (f32[16,8,128]{2,1,0:T(8,128)S(1)}, f32[16,8,128]{2,1,0:T(8,128)}, u32[]{:S(2)}) copy-start(f32[16,8,128]{2,1,0:T(8,128)} %constant.23.clone.cos_ref) | copy-start | bytes 196612
  9.3 104.1 %copy-start.9 = (bf16[32,128]{1,0:T(8,128)(2,1)S(1)}, bf16[32,128]{1,0:T(8,128)(2,1)}, u32[]{:S(2)}) copy-start(bf16[32,128]{1,0:T(8,128)(2,1)} %constant.26.clone.weight_ref) | copy-start | bytes 24580
where the time goes:
time: 119 us
  Pallas kernels  113 us (95%)
  local copies, waits for them, and re-layouts  5.59 us (5%)
    pallas_call x1, Pallas kernels, local(): pl.pallas_call(exchange_kernel, out_shape=jax.ShapeDtypeStruct((NY, CHUNK...  104 us
    pallas_call x1, Pallas kernels, local(): pl.pallas_call(invert_kernel, out_shape=jax.ShapeDtypeStruct((8, 4, 128,...  5.75 us
    unnamed x23, local copies, waits for them, and re-layouts  5.59 us
    pallas_call x1, Pallas kernels, local(): pl.pallas_call(whiten_kernel, out_shape=(jax.ShapeDtypeStruct((NY, CHUNKS...  3.01 us

commit v1 on v0

--- a/solution.py
+++ b/solution.py
@@ -17,6 +17,8 @@
 EPSILON = 1e-06
 NX, NZ, NY = 4, 8, 4
 CHUNKS = 4
+RINGS = 3
+ORDER = (0, 3, 1, 2)
 SLOTS = 32
 MIB = 1 << 20
 
@@ -105,17 +107,10 @@
     need_ref[...] = jnp.broadcast_to(need, (8, 128))
 
 
-def exchange_kernel(
-    white_ref,
-    need_ref,
-    pairs_ref,
-    stacked_ref,
-    *scratch,
-):
-    ring, chosen = scratch[:CHUNKS], scratch[CHUNKS : 2 * CHUNKS]
-    picked, sides, cross, table, lookup, need_sem, table_sem, own_sem, y_sem, z_sem, x_sem, c_sem, keep_sem = scratch[
-        2 * CHUNKS :
-    ]
+def exchange_kernel(white_ref, need_ref, pairs_ref, stacked_ref, *scratch):
+    ring, chosen = scratch[:RINGS], scratch[RINGS : RINGS + CHUNKS]
+    group, picked, bounce, sides, cross, table, lookup = scratch[RINGS + CHUNKS : RINGS + CHUNKS + 7]
+    need_sem, table_sem, own_sem, y_sem, z_sem, x_sem, g_sem, c_sem, keep_sem = scratch[RINGS + CHUNKS + 7 :]
     sta, q = lax.axis_index("sta"), lax.axis_index("seg")
     x, z, core = sta // 16, sta // 2 % 8, sta % 2
 
@@ -127,8 +122,8 @@
         return (sta, (q + dy) % NY)
 
     row_peers = [(d, f) for d in range(NX) for f in range(2) if (d, f) != (0, 0)]
-    targets = [along(r) for r in range(1, NY)] + [at(0, 1, 0), at(0, NZ - 1, 0)]
-    targets += [at(d, 0, f) for d, f in row_peers]
+    up, down, right, left = at(0, 1, 0), at(0, NZ - 1, 0), at(1, 0, 0), at(NX - 1, 0, 0)
+    targets = [along(r) for r in range(1, NY)] + [up, down] + [at(d, 0, f) for d, f in row_peers]
     barrier = pltpu.get_barrier_semaphore()
     for target in targets:
         pl.semaphore_signal(barrier, inc=1, device_id=target, device_id_type=MESH)
@@ -144,35 +139,42 @@
         started.append(copy)
         return copy
 
-    own = []
-    y_in = [[] for _ in range(CHUNKS)]
-    for c in range(CHUNKS):
-        for r in range(1, NY):
-            y_in[c].append(
-                send(white_ref.at[(q + r) % NY, c], ring[c].at[0, r], y_sem.at[c, r], along(r))
-            )
-        copy = pltpu.make_async_copy(white_ref.at[q, c], ring[c].at[0, 0], own_sem.at[c])
-        copy.start()
-        own.append(copy)
+    def home(c):
+        return ring[c].at[0] if c < RINGS else group.at[0, 0]
+
+    own, y_in = {}, {}
+    for c in ORDER:
+        y_in[c] = [
+            send(white_ref.at[(q + r) % NY, c], home(c).at[r], y_sem.at[c, r], along(r)) for r in range(1, NY)
+        ]
+        own[c] = pltpu.make_async_copy(white_ref.at[q, c], home(c).at[0], own_sem.at[c])
+        own[c].start()
     need_in = [
         send(need_ref, table.at[d * 2 + f], need_sem.at[d * 2 + f], at(d, 0, f)) for d, f in row_peers
     ]
     table[0] = need_ref[...]
 
-    def gather_ring(c):
+    def home_ready(c):
         own[c].wait()
         for copy in y_in[c]:
             copy.wait_recv()
-        for t in range(1, 5):
-            copies = []
-            if t < 4 or c % 2 == 0:
-                copies.append(send(ring[c].at[t - 1], ring[c].at[t], z_sem.at[c, t], at(0, 1, 0)))
-            if t < 4 or c % 2 == 1:
-                copies.append(
-                    send(ring[c].at[(9 - t) % 8], ring[c].at[8 - t], z_sem.at[c, 8 - t], at(0, NZ - 1, 0))
-                )
-            for copy in copies:
-                copy.wait_recv()
+
+    def landed(copies):
+        for copy in copies:
+            copy.wait_recv()
+
+    hops = {}
+
+    def hop(c, t):
+        if t == 1:
+            home_ready(c)
+        else:
+            landed(hops[c, t - 1])
+        hops[c, t] = []
+        if t < 4 or c % 2 == 0:
+            hops[c, t].append(send(ring[c].at[t - 1], ring[c].at[t], z_sem.at[c, t], up))
+        if t < 4 or c % 2 == 1:
+            hops[c, t].append(send(ring[c].at[(9 - t) % 8], ring[c].at[8 - t], z_sem.at[c, 8 - t], down))
 
     def pick(c):
         def one(slot, carry):
@@ -181,27 +183,84 @@
                 picked[c, slot, dz] = ring[c][dz, :, block]
             return carry
 
+        landed(hops[c, 4])
         lax.fori_loop(0, 2 * NX, one, 0)
         chosen[c][0] = picked[c, 0]
 
+    arrivals, relays = {}, {}
+
     def spread(c):
-        return [
-            send(picked.at[c, d * 2 + f], chosen[c].at[(NX - d) % NX * 2 + f], x_sem.at[c, d * 2 + f], at(-d, 0, f))
-            for d, f in row_peers
+        relays[c] = [
+            send(picked.at[c, 4], bounce.at[c, 0], x_sem.at[c, 0], right),
+            send(picked.at[c, 5], bounce.at[c, 1], x_sem.at[c, 1], left),
+        ]
+        arrivals[c] = [
+            send(picked.at[c, 6], chosen[c].at[2], x_sem.at[c, 2], right),
+            send(picked.at[c, 2], chosen[c].at[6], x_sem.at[c, 3], left),
+            send(picked.at[c, 7], chosen[c].at[3], x_sem.at[c, 4], at(1, 0, 1)),
+            send(picked.at[c, 3], chosen[c].at[7], x_sem.at[c, 5], at(NX - 1, 0, 1)),
+            send(picked.at[c, 1], chosen[c].at[1], x_sem.at[c, 6], at(0, 0, 1)),
+        ]
+
+    def forward(c):
+        relays[c][0].wait_recv()
+        arrivals[c].append(send(bounce.at[c, 0], chosen[c].at[4], x_sem.at[c, 7], right))
+        relays[c][1].wait_recv()
+        arrivals[c].append(send(bounce.at[c, 1], chosen[c].at[5], x_sem.at[c, 8], at(NX - 1, 0, 1)))
+
+    last = CHUNKS - 1
+    steps = {}
+
+    def group_start():
+        home_ready(last)
+        steps["x"] = [
+            send(group.at[0, 0], group.at[0, 1], g_sem.at[0], right),
+            send(group.at[0, 0], group.at[0, 3], g_sem.at[1], left),
+        ]
+
+    def group_across():
+        steps["x"][0].wait_recv()
+        one = send(group.at[0, 1, 0:2], group.at[0, 2, 0:2], g_sem.at[2], right)
+        steps["x"][1].wait_recv()
+        steps[0] = [one, send(group.at[0, 3, 2:4], group.at[0, 2, 2:4], g_sem.at[3], left)]
+
+    def group_hop(t):
+        landed(steps[t - 1])
+        if t < 4:
+            parts = (slice(0, 4), slice(0, 4))
+        else:
+            parts = (slice(0, 2), slice(2, 4))
+        steps[t] = [
+            send(group.at[t - 1, parts[0]], group.at[t, parts[0]], g_sem.at[2 * t + 2], up),
+            send(group.at[(9 - t) % 8, parts[1]], group.at[8 - t, parts[1]], g_sem.at[2 * t + 3], down),
+        ]
+
+    def group_pick():
+        def one(dx, carry):
+            for dz in range(NZ):
+                source = ((x - dx) % NX * NZ + (z - dz) % NZ) * 2 + core
+                picked[last, dx, dz] = group[dz, dx, :, lookup[1, 0, source]]
+                chosen[last][dx * 2, dz] = group[dz, dx, :, lookup[0, 0, source]]
+            return carry
+
+        landed(steps[4])
+        lax.fori_loop(0, NX, one, 0)
+        arrivals[last] = [
+            send(picked.at[last, d], chosen[last].at[2 * d + 1], g_sem.at[12 + d], at(0, 0, 1)) for d in range(NX)
         ]
 
     row = lax.broadcasted_iota(jnp.int32, (8, 128), 0)
-    left = lax.broadcasted_iota(jnp.int32, (8, 128), 1) < 64
+    first_half = lax.broadcasted_iota(jnp.int32, (8, 128), 1) < 64
 
     def prepare(c):
         def one(step, carry):
             b, r = step // NY, step % NY
-            both = ring[c][0, r, b].astype(F32)
+            both = home(c)[r, b].astype(F32)
             for g in range(2):
                 value = both[8 * g : 8 * g + 8]
                 turned = pltpu.roll(value, 64, 1)
                 for part, side in enumerate(
-                    (jnp.where(left, value, -turned), jnp.where(left, turned, value))
+                    (jnp.where(first_half, value, -turned), jnp.where(first_half, turned, value))
                 ):
                     for i in range(4):
                         only = jnp.where(row // 2 == i, side, 0.0)
@@ -210,6 +269,8 @@
             return carry
 
         lax.fori_loop(0, 4 * NY, one, 0)
+
+    kept, handed = [], []
 
     def multiply(c):
         def one(slot, carry):
@@ -229,52 +290,58 @@
             cross[c, slot] = jnp.concatenate(rows, axis=0).astype(BF16)
             return carry
 
+        landed(arrivals[c])
         lax.fori_loop(0, SLOTS, one, 0)
-
-    last = []
-
-    def hand_over(c):
         for r in range(1, NY):
-            last.append(
-                send(
-                    cross.at[c, pl.ds((q + r) % NY * 8, 8)],
-                    stacked_ref.at[q, c],
-                    c_sem.at[c, r],
-                    along(r),
-                )
-            )
+            part = cross.at[c, pl.ds((q + r) % NY * 8, 8)]
+            handed.append(send(part, stacked_ref.at[q, c], c_sem.at[c, r], along(r)))
         copy = pltpu.make_async_copy(cross.at[c, pl.ds(q * 8, 8)], stacked_ref.at[q, c], keep_sem.at[c])
         copy.start()
-        return copy
-
-    kept = []
-    x_in = {}
-
-    def finish(c):
-        prepare(c)
-        for copy in x_in[c]:
-            copy.wait_recv()
-        multiply(c)
-        kept.append(hand_over(c))
-
-    gather_ring(0)
-    for copy in need_in:
-        copy.wait_recv()
+        kept.append(copy)
+
+    hop(0, 1)
+    group_start()
+    hop(1, 1)
+    hop(0, 2)
+    landed(need_in)
     copy = pltpu.make_async_copy(table, lookup, table_sem)
     copy.start()
     copy.wait()
-    for c in range(CHUNKS):
-        if c:
-            gather_ring(c)
-        pick(c)
-        x_in[c] = spread(c)
-        if c:
-            finish(c - 1)
-    finish(CHUNKS - 1)
+    group_across()
+    hop(2, 1)
+    hop(1, 2)
+    hop(0, 3)
+    hop(2, 2)
+    hop(1, 3)
+    hop(0, 4)
+    group_hop(1)
+    pick(0)
+    spread(0)
+    hop(2, 3)
+    hop(1, 4)
+    pick(1)
+    forward(0)
+    spread(1)
+    hop(2, 4)
+    group_hop(2)
+    prepare(0)
+    pick(2)
+    group_hop(3)
+    multiply(0)
+    prepare(1)
+    forward(1)
+    spread(2)
+    group_hop(4)
+    multiply(1)
+    prepare(last)
+    forward(2)
+    group_pick()
+    multiply(last)
+    prepare(2)
+    multiply(2)
     for copy in kept:
         copy.wait()
-    for copy in last:
-        copy.wait_recv()
+    landed(handed)
     for copy in started:
         copy.wait_send()
 
@@ -330,9 +397,11 @@
         in_specs=[vmem(), vmem(), pl.BlockSpec(memory_space=pltpu.SMEM)],
         out_specs=pl.BlockSpec(memory_space=pl.ANY),
         scratch_shapes=[
-            *[pltpu.VMEM((NZ, NY, 4, 16, 128), BF16)] * CHUNKS,
+            *[pltpu.VMEM((NZ, NY, 4, 16, 128), BF16)] * RINGS,
             *[pltpu.VMEM((2 * NX, NZ, NY, 16, 128), BF16)] * CHUNKS,
+            pltpu.VMEM((NZ, NX, NY, 4, 16, 128), BF16),
             pltpu.VMEM((CHUNKS, 2 * NX, NZ, NY, 16, 128), BF16),
+            pltpu.VMEM((RINGS, 2, NZ, NY, 16, 128), BF16),
             pltpu.VMEM((4, 2, 4, 8, 8, 128), F32),
             pltpu.VMEM((CHUNKS, SLOTS, 32, 128), BF16),
             pltpu.VMEM((2 * NX, 8, 128), jnp.int32),
@@ -341,8 +410,9 @@
             dma(()),
             dma((CHUNKS,)),
             dma((CHUNKS, NY, 2)),
-            dma((CHUNKS, NZ, 2)),
-            dma((CHUNKS, 2 * NX, 2)),
+            dma((RINGS, NZ, 2)),
+            dma((RINGS, 9, 2)),
+            dma((16, 2)),
             dma((CHUNKS, NY, 2)),
             dma((CHUNKS,)),
         ],

time: 119 us -> 92 us (0.77)
  Pallas kernels: 113 us -> 85.4 us
    pallas_call x1, Pallas kernels: 104 us -> 76.7 us  [local(): pl.pallas_call(exchange_kernel, out_shape=jax.ShapeDtypeStruct((NY, CHUNK...]
where the time goes in v1:
time: 92 us; the launch traced here: 91.8 us
  Pallas kernels  85.4 us (93%)
  local copies, waits for them, and re-layouts  5.59 us (6%)
    pallas_call x1, Pallas kernels, local(): pl.pallas_call(exchange_kernel, out_shape=jax.ShapeDtypeStruct((NY, CHUNK...  76.7 us
    pallas_call x1, Pallas kernels, local(): pl.pallas_call(invert_kernel, out_shape=jax.ShapeDtypeStruct((8, 4, 128,...  5.75 us
    unnamed x23, local copies, waits for them, and re-layouts  5.59 us
    pallas_call x1, Pallas kernels, local(): pl.pallas_call(whiten_kernel, out_shape=(jax.ShapeDtypeStruct((NY, CHUNKS...  3.01 us

profile of v1, /device:TPU:1, one launch (start us, length us, event | category | flops | bytes accessed | tf_op | source)
XLA Modules:
  0.0 91.8 jit_solution(9782427547428065967)
XLA Ops:
  0.7 0.0 copy-start.10
  0.7 0.7 copy-done.10
  1.3 0.1 copy.14.pairs_ref
  1.4 0.0 copy-start
  1.4 1.0 %copy-done = f32[16,2,4096]{2,1,0:T(2,128)S(1)} copy-done((f32[16,2,4096]{2,1,0:T(2,128)S(1)}, f32[16,2,4096]{2,1,0:T(2,128)}, u32[]{:S(2)}) %copy-start) | copy-done | bytes 524312
  2.5 0.0 copy-start.1
  2.5 1.0 %copy-done.1 = f32[512,256]{1,0:T(8,128)S(1)} copy-done((f32[512,256]{1,0:T(8,128)S(1)}, f32[512,256]{1,0:T(8,128)}, u32[]{:S(2)}) %copy-start.1) | copy-done | bytes 524312
  3.5 0.0 copy-start.4
  3.5 0.9 copy-done.4
  4.4 0.0 copy-start.5
  4.4 0.9 copy-done.5
  5.3 0.0 copy-start.6
  5.3 0.9 copy-done.6
  6.2 3.0 %whiten.1 = (bf16[4,4,4,16,128]{4,3,2,1,0:T(8,128)(2,1)S(1)}, s32[8,128]{1,0:T(8,128)S(1)}) custom-call(f32[1024,128]{1,0:T(8,128)S(1)} %bitcast.10, s32[32,2]{1,0:T(8,128)S(1)} %copy.14.pairs_ref, f32[512,256]{1,0:T(8,128)S(1)} %copy-done.1, f32[256,128]{1,0:T(8,128)S(1)} %copy-done.6, f32[256,128]{1,0:T(8,128)S(1)} %copy-done.5, f32[256,128]{1,0:T(8,128)S(1)} %copy-done.4), custom_call_target="tpu_custom_call" | custom-call | tf_op jit(solution)/shard_map/whiten/pallas_call | solution.py:382
  9.2 0.0 copy-start.2
  9.2 0.0 copy-start.3
  9.3 0.0 copy-start.7
  9.3 0.0 copy-start.8
  9.3 0.0 copy-start.9
  9.3 76.7 %exchange.1.stacked_ref = bf16[4,4,8,32,128]{4,3,2,1,0:T(8,128)(2,1)S(1)} custom-call(bf16[4,4,4,16,128]{4,3,2,1,0:T(8,128)(2,1)S(1)} %get-tuple-element.7.white_ref, s32[8,128]{1,0:T(8,128)S(1)} %get-tuple-element.8.need_ref, s32[32,2]{1,0:T(8,128)S(1)} %copy.14.pairs_ref), custom_call_target="tpu_custom_call" | custom-call | tf_op jit(solution)/shard_map/exchange/pallas_call | solution.py:394
  86.0 0.0 copy-done.2
  86.0 0.0 copy-done.3
  86.0 0.0 copy-done.7
  86.0 0.0 copy-done.8
  86.0 0.0 copy-done.9
  86.0 5.7 %invert.1 = bf16[8,4,128,128]{3,2,1,0:T(8,128)(2,1)} custom-call(s32[1]{0:T(128)S(6)} %copy.17.counts_ref, bf16[4,4,8,32,128]{4,3,2,1,0:T(8,128)(2,1)S(1)} %exchange.1.stacked_ref, bf16[256,256]{1,0:T(8,128)(2,1)S(1)} %copy-done.3, f32[16,8,128]{2,1,0:T(8,128)S(1)} %copy-done.8, f32[16,8,128]{2,1,0:T(8,128)S(1)} %copy-done.7, ...), custom_call_target="tpu_custom_call" | custom-call | tf_op jit(solution)/shard_map/invert/pallas_call | solution.py:425
Async XLA Ops:
  0.7 0.7 copy-start.10
  1.4 1.0 %copy-start = (f32[16,2,4096]{2,1,0:T(2,128)S(1)}, f32[16,2,4096]{2,1,0:T(2,128)}, u32[]{:S(2)}) copy-start(f32[16,2,4096]{2,1,0:T(2,128)} %param.12) | copy-start | bytes 1572868
  2.5 1.0 %copy-start.1 = (f32[512,256]{1,0:T(8,128)S(1)}, f32[512,256]{1,0:T(8,128)}, u32[]{:S(2)}) copy-start(f32[512,256]{1,0:T(8,128)} %constant.18.clone.outer_ref) | copy-start | bytes 1572868
  3.5 0.9 copy-start.4
  4.4 0.9 copy-start.5
  5.3 0.9 copy-start.6
  9.2 76.7 %copy-start.2 = (bf16[128,768]{1,0:T(8,128)(2,1)S(1)}, bf16[128,768]{1,0:T(8,128)(2,1)}, u32[]{:S(2)}) copy-start(bf16[128,768]{1,0:T(8,128)(2,1)} %constant.25.clone.outer_ref) | copy-start | bytes 589828
  9.2 76.7 %copy-start.3 = (bf16[256,256]{1,0:T(8,128)(2,1)S(1)}, bf16[256,256]{1,0:T(8,128)(2,1)}, u32[]{:S(2)}) copy-start(bf16[256,256]{1,0:T(8,128)(2,1)} %constant.22.clone.inner_ref) | copy-start | bytes 393220
  9.3 76.7 %copy-start.7 = (f32[16,8,128]{2,1,0:T(8,128)S(1)}, f32[16,8,128]{2,1,0:T(8,128)}, u32[]{:S(2)}) copy-start(f32[16,8,128]{2,1,0:T(8,128)} %constant.24.clone.sin_ref) | copy-start | bytes 196612
  9.3 76.7 %copy-start.8 = (f32[16,8,128]{2,1,0:T(8,128)S(1)}, f32[16,8,128]{2,1,0:T(8,128)}, u32[]{:S(2)}) copy-start(f32[16,8,128]{2,1,0:T(8,128)} %constant.23.clone.cos_ref) | copy-start | bytes 196612
  9.3 76.7 %copy-start.9 = (bf16[32,128]{1,0:T(8,128)(2,1)S(1)}, bf16[32,128]{1,0:T(8,128)(2,1)}, u32[]{:S(2)}) copy-start(bf16[32,128]{1,0:T(8,128)(2,1)} %constant.26.clone.weight_ref) | copy-start | bytes 24580

commit v2 on v1

v2 whole, which is shorter than its diff:
```python
import functools
import math

import jax
import jax.numpy as jnp
import ml_dtypes
import numpy as np
from jax import lax
from jax.experimental import pallas as pl
from jax.experimental.pallas import tpu as pltpu
from jax.sharding import PartitionSpec as P

MESH = pl.DeviceIdType.MESH
F32 = jnp.float32
BF16 = jnp.bfloat16
HIGHEST = lax.Precision.HIGHEST
EPSILON = 1e-06
NX, NZ, NY = 4, 8, 4
CHUNKS = 4
RINGS = 3
ORDER = (0, 3, 1, 2)
PLACES = (0, 1, 7, 2, 6, 3, 5, 4)
NEAR = 5
UNROLL = 2
SLOTS = 32
STEP = 4
MIB = 1 << 20


def split_high(table):
    high = table.astype(ml_dtypes.bfloat16)
    return high, (table - high.astype(np.float64)).astype(ml_dtypes.bfloat16)


def forward_tables():
    a = np.arange(32)
    outer = np.zeros((2, 16, 2, 4, 2, 4, 32, 2))
    for c in range(16):
        for e in range(2):
            angle = 2 * np.pi * (a * (2 * c + e) % 32) / 32
            for g in range(2):
                for j in range(4):
                    outer[0, c, g, j, e, j, :, g] = np.cos(angle)
                    outer[1, c, g, j, e, j, :, g] = -np.sin(angle)
    k = np.broadcast_to(2 * np.arange(16)[:, None, None] + np.arange(2), (16, 8, 2)).reshape(256)
    twist = 2 * np.pi * (k[:, None] * np.arange(128)) / 4096
    inner = 2 * np.pi * (np.arange(128)[:, None] * np.arange(64) % 128) / 128
    cos, sin = np.cos(inner), np.sin(inner)
    inner = np.concatenate([np.concatenate([cos, -sin], 1), np.concatenate([sin, cos], 1)], 0)
    return tuple(
        t.astype(np.float32) for t in (outer.reshape(512, 256), np.cos(twist), np.sin(twist), inner)
    )


def inverse_tables():
    inner = 2 * np.pi * (np.arange(64)[:, None] * np.arange(128) % 128) / 128
    cos, sin = np.cos(inner) / 64, np.sin(inner) / 64
    inner = np.concatenate([np.concatenate([cos, sin], 1), np.concatenate([-sin, cos], 1)], 0)
    inner = np.concatenate(split_high(inner), 0)
    k = np.broadcast_to(2 * np.arange(16)[:, None, None] + np.arange(2), (16, 4, 2)).reshape(16, 8)
    twist = 2 * np.pi * (k[:, :, None] * np.arange(128)) / 4096
    outer = np.zeros((32, 4, 2, 16, 4, 2))
    u = np.arange(32)
    for c in range(16):
        for e in range(2):
            angle = 2 * np.pi * (u * (2 * c + e) % 32) / 32
            for j in range(4):
                outer[:, j, 0, c, j, e] = np.cos(angle)
                outer[:, j, 1, c, j, e] = -np.sin(angle)
    high, low = split_high(outer.reshape(128, 256))
    outer = np.concatenate([high, high, low], 1)
    weight = np.ones((32, 128))
    weight[::2, 0] = 0.5
    return (
        inner,
        np.cos(twist).astype(np.float32),
        np.sin(twist).astype(np.float32),
        outer,
        weight.astype(ml_dtypes.bfloat16),
    )


def whiten(x_ref, outer_ref, cos_ref, sin_ref, inner_ref, white_ref):
    x = x_ref[...].reshape(16, 8, 8, 128)
    total = jnp.sum(x, axis=1)
    total = total + pltpu.roll(total, 4, 1)
    total = total + pltpu.roll(total, 2, 1)
    mean = jnp.sum(total, axis=-1, keepdims=True) * (1.0 / 4096)
    x = (x - mean[:, None]).reshape(4, 256, 128)
    row = lax.broadcasted_iota(jnp.int32, (2, 8, 128), 1)
    lane = lax.broadcasted_iota(jnp.int32, (2, 8, 128), 2)
    for half in range(2):
        both = jnp.concatenate([x[2 * half], x[2 * half + 1]], axis=1)
        section = jnp.dot(outer_ref[...], both, precision=HIGHEST, preferred_element_type=F32)
        cos, sin = cos_ref[...], sin_ref[...]
        for b in range(2):
            real = section[:256, 128 * b : 128 * b + 128]
            imag = section[256:, 128 * b : 128 * b + 128]
            turned = jnp.concatenate([real * cos + imag * sin, imag * cos - real * sin], axis=1)
            spec = jnp.dot(turned, inner_ref[...], precision=HIGHEST, preferred_element_type=F32)
            spec = spec.reshape(16, 2, 8, 128)
            power = jnp.sum(spec * spec, axis=0)
            power = power + jnp.where(row % 2 == 0, pltpu.roll(power, 7, 1), pltpu.roll(power, 1, 1))
            power = power + jnp.where(lane % 2 == 0, pltpu.roll(power, 127, 2), pltpu.roll(power, 1, 2))
            power = power + pltpu.roll(power, 64, 2)
            white = spec * (1.0 / jnp.sqrt(power * (1.0 / 64) + EPSILON))
            white_ref[:, :, 2 * half + b] = white.reshape(4, 4, 16, 128).astype(BF16)


def blocks_named(partner):
    row = lax.broadcasted_iota(jnp.int32, (SLOTS, SLOTS), 0)
    column = lax.broadcasted_iota(jnp.int32, (SLOTS, SLOTS), 1)
    partner = jnp.sum(jnp.where(row == column, partner, 0), axis=1, keepdims=True)
    source = lax.broadcasted_iota(jnp.int32, (SLOTS, 128), 1)
    named = jnp.sum(jnp.where(partner // 4 == source, partner % 4, 0), axis=0, keepdims=True)
    return jnp.broadcast_to(named, (8, 128))


def exchange_kernel(
    rows_ref, outer_ref, cos_ref, sin_ref, inner_ref, partners_ref, pairs_ref, stacked_ref, *scratch
):
    chosen, rings = scratch[:CHUNKS], scratch[CHUNKS : CHUNKS + RINGS + 1]
    near, far = rings[:2]
    load, scratch = scratch[CHUNKS + RINGS + 1 : CHUNKS + RINGS + 6], scratch[CHUNKS + RINGS + 6 :]
    white_ref, need_ref, group, picked, bounce, sides, cross, table, lookup = scratch[:9]
    load_sem, need_sem, table_sem, own_sem, y_sem, z_sem, x_sem, g_sem, c_sem, keep_sem = scratch[9:]
    sta, q = lax.axis_index("sta"), lax.axis_index("seg")
    x, z, core = sta // 16, sta // 2 % 8, sta % 2

    def at(dx, dz, flip):
        other = core if flip == 0 else 1 - core
        return (((x + dx) % NX * NZ + (z + dz) % NZ) * 2 + other, q)

    def along(dy):
        return (sta, (q + dy) % NY)

    row_peers = [(d, f) for d in range(NX) for f in range(2) if (d, f) != (0, 0)]
    up, down, right, left = at(0, 1, 0), at(0, NZ - 1, 0), at(1, 0, 0), at(NX - 1, 0, 0)
    targets = [along(r) for r in range(1, NY)] + [up, down] + [at(d, 0, f) for d, f in row_peers]
    barrier = pltpu.get_barrier_semaphore()
    for target in targets:
        pl.semaphore_signal(barrier, inc=1, device_id=target, device_id_type=MESH)
    loads = [
        pltpu.make_async_copy(source, target, load_sem.at[i])
        for i, (source, target) in enumerate(zip((rows_ref, outer_ref, cos_ref, sin_ref, inner_ref), load))
    ]
    for copy in loads:
        copy.start()
    need_ref[...] = blocks_named(partners_ref[1:2])
    table[0] = need_ref[...]
    for copy in loads:
        copy.wait()
    whiten(*load, white_ref)
    pl.semaphore_wait(barrier, len(targets))

    started = []

    def send(source, destination, sems, target):
        copy = pltpu.make_async_remote_copy(
            source, destination, sems.at[0], sems.at[1], device_id=target, device_id_type=MESH
        )
        copy.start()
        started.append(copy)
        return copy

    def ring(c, dz):
        place = PLACES.index(dz)
        if c:
            return rings[c + 1].at[place]
        return near.at[place] if place < NEAR else far.at[place - NEAR]

    def home(c):
        return ring(c, 0) if c < RINGS else group.at[0, 0]

    own, y_in = {}, {}
    for c in ORDER:
        y_in[c] = [
            send(white_ref.at[(q + r) % NY, c], home(c).at[r], y_sem.at[c, r], along(r)) for r in range(1, NY)
        ]
        own[c] = pltpu.make_async_copy(white_ref.at[q, c], home(c).at[0], own_sem.at[c])
        own[c].start()
    need_in = [
        send(need_ref, table.at[d * 2 + f], need_sem.at[d * 2 + f], at(d, 0, f)) for d, f in row_peers
    ]

    def home_ready(c):
        own[c].wait()
        for copy in y_in[c]:
            copy.wait_recv()

    def landed(copies):
        for copy in copies:
            copy.wait_recv()

    hops = {}

    def hop(c, t):
        if t == 1:
            home_ready(c)
        else:
            landed(hops[c, t - 1])
        hops[c, t] = []
        if t < 4 or c % 2 == 0:
            hops[c, t].append(send(ring(c, t - 1), ring(c, t), z_sem.at[c, t], up))
        if t < 4 or c % 2 == 1:
            hops[c, t].append(send(ring(c, (9 - t) % 8), ring(c, 8 - t), z_sem.at[c, 8 - t], down))

    def pick(c, part):
        def one(slot, carry):
            for place in range(*part):
                dz = PLACES[place]
                block = lookup[slot, 0, (x * NZ + (z - dz) % NZ) * 2 + core]
                picked[c, slot, place] = ring(c, dz)[:, block]
            return carry

        if part[1] == NZ:
            landed(hops[c, 4])
        lax.fori_loop(0, 2 * NX, one, 0)
        chosen[c][0, part[0] : part[1]] = picked[c, 0, part[0] : part[1]]

    arrivals, relays = {c: [] for c in range(CHUNKS)}, {}

    def spread(c, part):
        some = slice(*part)
        sems = x_sem.at[c, int(part[0] > 0)]

        def pass_on(slot, target, sem, device):
            return send(picked.at[c, slot, some], target.at[some], sems.at[sem], device)

        relays[c, part] = [
            pass_on(4, bounce.at[c, 0], 0, right),
            pass_on(5, bounce.at[c, 1], 1, left),
        ]
        arrivals[c] += [
            pass_on(6, chosen[c].at[2], 2, right),
            pass_on(2, chosen[c].at[6], 3, left),
            pass_on(7, chosen[c].at[3], 4, at(1, 0, 1)),
            pass_on(3, chosen[c].at[7], 5, at(NX - 1, 0, 1)),
            pass_on(1, chosen[c].at[1], 6, at(0, 0, 1)),
        ]

    def forward(c, part):
        some = slice(*part)
        sems = x_sem.at[c, int(part[0] > 0)]
        relays[c, part][0].wait_recv()
        arrivals[c].append(send(bounce.at[c, 0, some], chosen[c].at[4, some], sems.at[7], right))
        relays[c, part][1].wait_recv()
        arrivals[c].append(send(bounce.at[c, 1, some], chosen[c].at[5, some], sems.at[8], at(NX - 1, 0, 1)))

    last = CHUNKS - 1
    steps = {}

    def group_start():
        home_ready(last)
        steps["x"] = [
            send(group.at[0, 0], group.at[0, 1], g_sem.at[0], right),
            send(group.at[0, 0], group.at[0, 3], g_sem.at[1], left),
        ]

    def group_across():
        steps["x"][0].wait_recv()
        one = send(group.at[0, 1, 0:2], group.at[0, 2, 0:2], g_sem.at[2], right)
        steps["x"][1].wait_recv()
        steps[0] = [one, send(group.at[0, 3, 2:4], group.at[0, 2, 2:4], g_sem.at[3], left)]

    def group_hop(t):
        landed(steps[t - 1])
        if t < 4:
            parts = (slice(0, 4), slice(0, 4))
        else:
            parts = (slice(0, 2), slice(2, 4))
        steps[t] = [
            send(group.at[t - 1, parts[0]], group.at[t, parts[0]], g_sem.at[2 * t + 2], up),
            send(group.at[(9 - t) % 8, parts[1]], group.at[8 - t, parts[1]], g_sem.at[2 * t + 3], down),
        ]

    def group_pick():
        def one(dx, carry):
            for place, dz in enumerate(PLACES):
                source = ((x - dx) % NX * NZ + (z - dz) % NZ) * 2 + core
                picked[last, dx, place] = group[dz, dx, :, lookup[1, 0, source]]
                chosen[last][dx * 2, place] = group[dz, dx, :, lookup[0, 0, source]]
            return carry

        landed(steps[4])
        lax.fori_loop(0, NX, one, 0)
        arrivals[last] += [
            send(picked.at[last, d], chosen[last].at[2 * d + 1], g_sem.at[12 + d], at(0, 0, 1)) for d in range(NX)
        ]

    row = lax.broadcasted_iota(jnp.int32, (8, 128), 0)
    first_half = lax.broadcasted_iota(jnp.int32, (8, 128), 1) < 64

    def prepare(c):
        def one(step, carry):
            b, r = step // NY, step % NY
            both = home(c)[r, b].astype(F32)
            for g in range(2):
                value = both[8 * g : 8 * g + 8]
                turned = pltpu.roll(value, 64, 1)
                for part, side in enumerate(
                    (jnp.where(first_half, value, -turned), jnp.where(first_half, turned, value))
                ):
                    for i in range(4):
                        only = jnp.where(row // 2 == i, side, 0.0)
                        only = only + pltpu.roll(only, 2, 0)
                        sides[side_of(c), b, part, i, r * 2 + g] = only + pltpu.roll(only, 4, 0)
            return carry

        lax.fori_loop(0, 4 * NY, one, 0)

    kept, handed = [], []

    def side_of(c):
        return int(c in (1, 2))

    def multiply(c):
        landed(arrivals[c])
        for r in (2, 1, 3, 0):
            base = (q + r) % NY * 8

            def one(n, carry):
                slot = base + n
                first = pairs_ref[0, slot] % 4
                partner = pairs_ref[1, slot] // 4
                dx, dz, flip = (x - partner // 16) % NX, (z - partner // 2 % 8) % NZ, (core + partner) % 2
                place = jnp.where(dz == 0, 0, jnp.where(dz <= 4, 2 * dz - 1, 2 * (NZ - dz)))
                second = chosen[c][dx * 2 + flip, place].astype(F32)
                rows = []
                for i in range(4):
                    straight = sides[side_of(c), first, 0, i, 0] * second[0, 0:8]
                    crossed = sides[side_of(c), first, 1, i, 0] * second[0, 0:8]
                    for g in range(1, 8):
                        part = second[g // 2, 8 * (g % 2) : 8 * (g % 2) + 8]
                        straight = straight + sides[side_of(c), first, 0, i, g] * part
                        crossed = crossed + sides[side_of(c), first, 1, i, g] * part
                    rows.append(straight + pltpu.roll(crossed, 64, 1))
                cross[c, slot] = jnp.concatenate(rows, axis=0).astype(BF16)
                return carry

            lax.fori_loop(0, 8, one, 0, unroll=UNROLL)
            part = cross.at[c, pl.ds(base, 8)]
            if r:
                handed.append(send(part, stacked_ref.at[q, c], c_sem.at[c, r], along(r)))
            else:
                copy = pltpu.make_async_copy(part, stacked_ref.at[q, c], keep_sem.at[c])
                copy.start()
                kept.append(copy)

    near_part, far_part, whole = (0, NEAR), (NEAR, NZ), (0, NZ)
    hop(0, 1)
    group_start()
    hop(1, 1)
    hop(0, 2)
    landed(need_in)
    copy = pltpu.make_async_copy(table, lookup, table_sem)
    copy.start()
    copy.wait()
    group_across()
    hop(2, 1)
    hop(1, 2)
    hop(0, 3)
    pick(0, near_part)
    spread(0, near_part)
    hop(2, 2)
    hop(1, 3)
    hop(0, 4)
    group_hop(1)
    pick(0, far_part)
    forward(0, near_part)
    spread(0, far_part)
    hop(2, 3)
    hop(1, 4)
    pick(1, whole)
    forward(0, far_part)
    spread(1, whole)
    hop(2, 4)
    group_hop(2)
    prepare(0)
    pick(2, whole)
    multiply(0)
    forward(1, whole)
    spread(2, whole)
    group_hop(3)
    prepare(1)
    prepare(last)
    multiply(1)
    group_hop(4)
    prepare(2)
    forward(2, whole)
    group_pick()
    multiply(last)
    multiply(2)
    for copy in kept:
        copy.wait()
    landed(handed)
    for copy in started:
        copy.wait_send()


def invert_kernel(counts_ref, stacked_ref, inner_ref, cos_ref, sin_ref, outer_ref, weight_ref, out_ref):
    for n in range(STEP):
        slot = lax.axis_index("seg") * 8 + pl.program_id(0) * STEP + n
        live = (slot < counts_ref[0]).astype(F32)
        cross = stacked_ref[:, :, n].reshape(16, 32, 128)
        cross = jnp.concatenate([cross[0:1] * weight_ref[...], cross[1:]], axis=0).reshape(512, 128)
        series = jnp.dot(jnp.concatenate([cross, cross], axis=1), inner_ref[...], preferred_element_type=F32)
        series = series.reshape(16, 4, 8, 256)
        cos, sin = cos_ref[...] * live, sin_ref[...] * live
        parts = []
        for i in range(4):
            real, imag = series[:, i, :, :128], series[:, i, :, 128:]
            turned = jnp.concatenate(
                [(real * cos - imag * sin).reshape(128, 128), (real * sin + imag * cos).reshape(128, 128)], axis=0
            )
            parts.append(turned)
        for pair in range(2):
            both = jnp.concatenate([parts[2 * pair], parts[2 * pair + 1]], axis=1)
            high = both.astype(BF16)
            low = (both - high.astype(F32)).astype(BF16)
            lags = jnp.dot(
                outer_ref[...], jnp.concatenate([high, low, high], axis=0), preferred_element_type=F32
            ).astype(BF16)
            out_ref[n, 2 * pair] = lags[:, :128]
            out_ref[n, 2 * pair + 1] = lags[:, 128:]


def vmem():
    return pl.BlockSpec(memory_space=pltpu.VMEM)


def local(traces, pair_blocks, pair_counts):
    stations, segs, length = traces.shape
    rows = traces.reshape(stations, segs, 32, 128).transpose(0, 2, 1, 3).reshape(1024, 128)
    dma = pltpu.SemaphoreType.DMA
    smem = pl.BlockSpec(memory_space=pltpu.SMEM)
    stacked = pl.pallas_call(
        exchange_kernel,
        out_shape=jax.ShapeDtypeStruct((NY, CHUNKS, 8, 32, 128), BF16),
        in_specs=[pl.BlockSpec(memory_space=pltpu.HBM)] * 5 + [vmem(), smem],
        out_specs=pl.BlockSpec(memory_space=pl.ANY),
        scratch_shapes=[
            *[pltpu.VMEM((2 * NX, NZ, NY, 16, 128), BF16)] * CHUNKS,
            pltpu.VMEM((NEAR, NY, 4, 16, 128), BF16),
            pltpu.VMEM((NZ - NEAR, NY, 4, 16, 128), BF16),
            *[pltpu.VMEM((NZ, NY, 4, 16, 128), BF16)] * (RINGS - 1),
            pltpu.VMEM((1024, 128), F32),
            pltpu.VMEM((512, 256), F32),
            pltpu.VMEM((256, 128), F32),
            pltpu.VMEM((256, 128), F32),
            pltpu.VMEM((256, 128), F32),
            pltpu.VMEM((NY, CHUNKS, 4, 16, 128), BF16),
            pltpu.VMEM((8, 128), jnp.int32),
            pltpu.VMEM((NZ, NX, NY, 4, 16, 128), BF16),
            pltpu.VMEM((CHUNKS, 2 * NX, NZ, NY, 16, 128), BF16),
            pltpu.VMEM((RINGS, 2, NZ, NY, 16, 128), BF16),
            pltpu.VMEM((2, 4, 2, 4, 8, 8, 128), F32),
            pltpu.VMEM((CHUNKS, SLOTS, 32, 128), BF16),
            pltpu.VMEM((2 * NX, 8, 128), jnp.int32),
            pltpu.SMEM((2 * NX, 8, 128), jnp.int32),
            dma((5,)),
            dma((2 * NX, 2)),
            dma(()),
            dma((CHUNKS,)),
            dma((CHUNKS, NY, 2)),
            dma((RINGS, NZ, 2)),
            dma((RINGS, 2, 9, 2)),
            dma((16, 2)),
            dma((CHUNKS, NY, 2)),
            dma((CHUNKS,)),
        ],
        compiler_params=pltpu.CompilerParams(
            collective_id=0, has_side_effects=True, vmem_limit_bytes=63 * MIB
        ),
        name="exchange",
    )(rows, *forward_tables(), pair_blocks.T, pair_blocks.T)
    whole = lambda *shape: pl.BlockSpec(shape, lambda p: (0,) * len(shape))
    lags = pl.pallas_call(
        invert_kernel,
        out_shape=jax.ShapeDtypeStruct((8, 4, 128, 128), BF16),
        grid=(8 // STEP,),
        in_specs=[
            smem,
            pl.BlockSpec((NY, CHUNKS, STEP, 32, 128), lambda p: (0, 0, p, 0, 0)),
            whole(256, 256),
            whole(16, 8, 128),
            whole(16, 8, 128),
            whole(128, 768),
            whole(32, 128),
        ],
        out_specs=pl.BlockSpec((STEP, 4, 128, 128), lambda p: (p, 0, 0, 0)),
        compiler_params=pltpu.CompilerParams(vmem_limit_bytes=32 * MIB),
        name="invert",
    )(pair_counts, stacked, *inverse_tables())
    return lags.reshape(8, 4, 32, 4, 128).transpose(0, 1, 3, 2, 4).reshape(8, 4, 4, length)


def solution(mesh):
    in_specs = (P("sta", "seg", None), P("sta", None), P("sta"))
    out_specs = P(("sta", "seg"), None, None, None)
    return jax.shard_map(local, mesh=mesh, in_specs=in_specs, out_specs=out_specs, check_vma=False)
```

time: 92 us -> 79.1 us (0.86)
  Pallas kernels: 85.4 us -> 77 us
  local copies, waits for them, and re-layouts: 5.59 us -> 1.25 us
    unnamed x23 -> x12, local copies, waits for them, and re-layouts: 5.59 us -> 1.25 us
    pallas_call x1, Pallas kernels: 76.7 us -> 73 us  [local(): pl.pallas_call(exchange_kernel, out_shape=jax.ShapeDtypeStruct((NY, CHUNK...]
    pallas_call x1 -> x0, Pallas kernels: 3.01 us -> none  [local(): pl.pallas_call(whiten_kernel, out_shape=(jax.ShapeDtypeStruct((NY, CHUNKS...]
    pallas_call x1, Pallas kernels: 5.75 us -> 3.9 us  [local(): pl.pallas_call(invert_kernel, out_shape=jax.ShapeDtypeStruct((8, 4, 128,...]
where the time goes in v2:
time: 79.1 us; the launch traced here: 79 us
  Pallas kernels  77 us (97%)
  local copies, waits for them, and re-layouts  1.25 us (2%)
    pallas_call x1, Pallas kernels, local(): pl.pallas_call(exchange_kernel, out_shape=jax.ShapeDtypeStruct((NY, CHUNK...  73 us
    pallas_call x1, Pallas kernels, local(): pl.pallas_call(invert_kernel, out_shape=jax.ShapeDtypeStruct((8, 4, 128,...  3.9 us

profile of v2, /device:TPU:1, one launch (start us, length us, event | category | flops | bytes accessed | tf_op | source)
XLA Modules:
  0.0 79.0 jit_solution(4397912546142126524)
XLA Ops:
  0.7 0.0 copy-start.1
  0.7 0.0 copy-start.2
  0.7 0.0 copy-start.3
  0.7 0.0 copy-start.4
  0.7 0.0 copy-start.5
  0.7 73.0 %exchange.1.stacked_ref = bf16[4,4,8,32,128]{4,3,2,1,0:T(8,128)(2,1)} custom-call(f32[1024,128]{1,0:T(8,128)} %bitcast.11, f32[512,256]{1,0:T(8,128)} %constant.18.clone.outer_ref, f32[256,128]{1,0:T(8,128)} %constant.19.clone.cos_ref, f32[256,128]{1,0:T(8,128)} %constant.20.clone.sin_ref, f32[256,128]{1,0:T(8,128)} %constant.21.clone.inner_ref, ...), custom_call_target="tpu_custom_call" | custom-call | tf_op jit(solution)/shard_map/exchange/pallas_call | solution.py:437
  73.8 0.0 copy-done.1
  73.8 0.0 copy-done.2
  73.8 0.0 copy-done.3
  73.8 0.0 copy-done.4
  73.8 0.0 copy-done.5
  73.8 0.0 copy-start
  73.8 1.2 %copy-done = bf16[4,4,8,32,128]{4,3,2,1,0:T(8,128)(2,1)S(1)} copy-done((bf16[4,4,8,32,128]{4,3,2,1,0:T(8,128)(2,1)S(1)}, bf16[4,4,8,32,128]{4,3,2,1,0:T(8,128)(2,1)}, u32[]{:S(2)}) %copy-start) | copy-done | bytes 1048600
  75.0 3.9 %invert.1 = bf16[8,4,128,128]{3,2,1,0:T(8,128)(2,1)} custom-call(s32[1]{0:T(128)S(6)} %copy.15.counts_ref, bf16[4,4,8,32,128]{4,3,2,1,0:T(8,128)(2,1)S(1)} %copy-done, bf16[256,256]{1,0:T(8,128)(2,1)S(1)} %copy-done.2, f32[16,8,128]{2,1,0:T(8,128)S(1)} %copy-done.4, f32[16,8,128]{2,1,0:T(8,128)S(1)} %copy-done.3, bf16[128,768]{1,0:T(8,128)(2,1)S(1)} %copy-done.1, ...), custom_call_target="tpu_custom_call" | custom-call | tf_op jit(solution)/shard_map/invert/pallas_call | solution.py:478
Async XLA Ops:
  0.7 73.1 %copy-start.1 = (bf16[128,768]{1,0:T(8,128)(2,1)S(1)}, bf16[128,768]{1,0:T(8,128)(2,1)}, u32[]{:S(2)}) copy-start(bf16[128,768]{1,0:T(8,128)(2,1)} %constant.25.clone.outer_ref) | copy-start | bytes 589828
  0.7 73.1 %copy-start.2 = (bf16[256,256]{1,0:T(8,128)(2,1)S(1)}, bf16[256,256]{1,0:T(8,128)(2,1)}, u32[]{:S(2)}) copy-start(bf16[256,256]{1,0:T(8,128)(2,1)} %constant.22.clone.inner_ref) | copy-start | bytes 393220
  0.7 73.1 %copy-start.3 = (f32[16,8,128]{2,1,0:T(8,128)S(1)}, f32[16,8,128]{2,1,0:T(8,128)}, u32[]{:S(2)}) copy-start(f32[16,8,128]{2,1,0:T(8,128)} %constant.24.clone.sin_ref) | copy-start | bytes 196612
  0.7 73.1 %copy-start.4 = (f32[16,8,128]{2,1,0:T(8,128)S(1)}, f32[16,8,128]{2,1,0:T(8,128)}, u32[]{:S(2)}) copy-start(f32[16,8,128]{2,1,0:T(8,128)} %constant.23.clone.cos_ref) | copy-start | bytes 196612
  0.7 73.1 %copy-start.5 = (bf16[32,128]{1,0:T(8,128)(2,1)S(1)}, bf16[32,128]{1,0:T(8,128)(2,1)}, u32[]{:S(2)}) copy-start(bf16[32,128]{1,0:T(8,128)(2,1)} %constant.26.clone.weight_ref) | copy-start | bytes 24580
  73.8 1.2 %copy-start = (bf16[4,4,8,32,128]{4,3,2,1,0:T(8,128)(2,1)S(1)}, bf16[4,4,8,32,128]{4,3,2,1,0:T(8,128)(2,1)}, u32[]{:S(2)}) copy-start(bf16[4,4,8,32,128]{4,3,2,1,0:T(8,128)(2,1)} %exchange.1.stacked_ref) | copy-start | bytes 3145732

commit v3 on v2

--- a/solution.py
+++ b/solution.py
@@ -21,9 +21,9 @@
 ORDER = (0, 3, 1, 2)
 PLACES = (0, 1, 7, 2, 6, 3, 5, 4)
 NEAR = 5
-UNROLL = 2
+UNROLL = 4
 SLOTS = 32
-STEP = 4
+STEP = 2
 MIB = 1 << 20
 
 
@@ -378,17 +378,17 @@
     group_hop(2)
     prepare(0)
     pick(2, whole)
+    group_hop(3)
     multiply(0)
     forward(1, whole)
     spread(2, whole)
-    group_hop(3)
     prepare(1)
     prepare(last)
+    group_hop(4)
     multiply(1)
-    group_hop(4)
-    prepare(2)
     forward(2, whole)
     group_pick()
+    prepare(2)
     multiply(last)
     multiply(2)
     for copy in kept:
@@ -470,7 +470,7 @@
             dma((CHUNKS,)),
         ],
         compiler_params=pltpu.CompilerParams(
-            collective_id=0, has_side_effects=True, vmem_limit_bytes=63 * MIB
+            collective_id=0, has_side_effects=True, vmem_limit_bytes=60 * MIB
         ),
         name="exchange",
     )(rows, *forward_tables(), pair_blocks.T, pair_blocks.T)

time: 79.1 us -> 77.6 us (0.981)
  Pallas kernels: 77 us -> 74.7 us
    pallas_call x1, Pallas kernels: 73 us -> 71 us  [local(): pl.pallas_call(exchange_kernel, out_shape=jax.ShapeDtypeStruct((NY, CHUNK...]
where the time goes in v3:
time: 77.6 us; the launch traced here: 76.7 us
  Pallas kernels  74.7 us (96%)
  local copies, waits for them, and re-layouts  1.25 us (2%)
    pallas_call x1, Pallas kernels, local(): pl.pallas_call(exchange_kernel, out_shape=jax.ShapeDtypeStruct((NY, CHUNK...  71 us
    pallas_call x1, Pallas kernels, local(): pl.pallas_call(invert_kernel, out_shape=jax.ShapeDtypeStruct((8, 4, 128,...  3.67 us

profile of v3, /device:TPU:1, one launch (start us, length us, event | category | flops | bytes accessed | tf_op | source)
XLA Modules:
  0.0 76.7 jit_solution(17480561561352744631)
XLA Ops:
  0.7 0.0 copy-start.1
  0.7 0.0 copy-start.2
  0.7 0.0 copy-start.3
  0.7 0.0 copy-start.4
  0.7 0.0 copy-start.5
  0.7 71.0 %exchange.1.stacked_ref = bf16[4,4,8,32,128]{4,3,2,1,0:T(8,128)(2,1)} custom-call(f32[1024,128]{1,0:T(8,128)} %bitcast.11, f32[512,256]{1,0:T(8,128)} %constant.18.clone.outer_ref, f32[256,128]{1,0:T(8,128)} %constant.19.clone.cos_ref, f32[256,128]{1,0:T(8,128)} %constant.20.clone.sin_ref, f32[256,128]{1,0:T(8,128)} %constant.21.clone.inner_ref, ...), custom_call_target="tpu_custom_call" | custom-call | tf_op jit(solution)/shard_map/exchange/pallas_call | solution.py:437
  71.8 0.0 copy-done.1
  71.8 0.0 copy-done.2
  71.8 0.0 copy-done.3
  71.8 0.0 copy-done.4
  71.8 0.0 copy-done.5
  71.8 0.0 copy-start
  71.8 1.2 %copy-done = bf16[4,4,8,32,128]{4,3,2,1,0:T(8,128)(2,1)S(1)} copy-done((bf16[4,4,8,32,128]{4,3,2,1,0:T(8,128)(2,1)S(1)}, bf16[4,4,8,32,128]{4,3,2,1,0:T(8,128)(2,1)}, u32[]{:S(2)}) %copy-start) | copy-done | bytes 1048600
  73.0 3.7 %invert.1 = bf16[8,4,128,128]{3,2,1,0:T(8,128)(2,1)} custom-call(s32[1]{0:T(128)S(6)} %copy.15.counts_ref, bf16[4,4,8,32,128]{4,3,2,1,0:T(8,128)(2,1)S(1)} %copy-done, bf16[256,256]{1,0:T(8,128)(2,1)S(1)} %copy-done.2, f32[16,8,128]{2,1,0:T(8,128)S(1)} %copy-done.4, f32[16,8,128]{2,1,0:T(8,128)S(1)} %copy-done.3, bf16[128,768]{1,0:T(8,128)(2,1)S(1)} %copy-done.1, ...), custom_call_target="tpu_custom_call" | custom-call | tf_op jit(solution)/shard_map/invert/pallas_call | solution.py:478
Async XLA Ops:
  0.7 71.1 %copy-start.1 = (bf16[128,768]{1,0:T(8,128)(2,1)S(1)}, bf16[128,768]{1,0:T(8,128)(2,1)}, u32[]{:S(2)}) copy-start(bf16[128,768]{1,0:T(8,128)(2,1)} %constant.25.clone.outer_ref) | copy-start | bytes 589828
  0.7 71.1 %copy-start.2 = (bf16[256,256]{1,0:T(8,128)(2,1)S(1)}, bf16[256,256]{1,0:T(8,128)(2,1)}, u32[]{:S(2)}) copy-start(bf16[256,256]{1,0:T(8,128)(2,1)} %constant.22.clone.inner_ref) | copy-start | bytes 393220
  0.7 71.1 %copy-start.3 = (f32[16,8,128]{2,1,0:T(8,128)S(1)}, f32[16,8,128]{2,1,0:T(8,128)}, u32[]{:S(2)}) copy-start(f32[16,8,128]{2,1,0:T(8,128)} %constant.24.clone.sin_ref) | copy-start | bytes 196612
  0.7 71.1 %copy-start.4 = (f32[16,8,128]{2,1,0:T(8,128)S(1)}, f32[16,8,128]{2,1,0:T(8,128)}, u32[]{:S(2)}) copy-start(f32[16,8,128]{2,1,0:T(8,128)} %constant.23.clone.cos_ref) | copy-start | bytes 196612
  0.7 71.1 %copy-start.5 = (bf16[32,128]{1,0:T(8,128)(2,1)S(1)}, bf16[32,128]{1,0:T(8,128)(2,1)}, u32[]{:S(2)}) copy-start(bf16[32,128]{1,0:T(8,128)(2,1)} %constant.26.clone.weight_ref) | copy-start | bytes 24580
  71.8 1.2 %copy-start = (bf16[4,4,8,32,128]{4,3,2,1,0:T(8,128)(2,1)S(1)}, bf16[4,4,8,32,128]{4,3,2,1,0:T(8,128)(2,1)}, u32[]{:S(2)}) copy-start(bf16[4,4,8,32,128]{4,3,2,1,0:T(8,128)(2,1)} %exchange.1.stacked_ref) | copy-start | bytes 3145732

commit v4 on v3

--- a/solution.py
+++ b/solution.py
@@ -163,6 +163,11 @@
         started.append(copy)
         return copy
 
+    def sent():
+        for copy in started:
+            copy.wait_send()
+        started.clear()
+
     def ring(c, dz):
         place = PLACES.index(dz)
         if c:
@@ -312,7 +317,7 @@
     kept, handed = [], []
 
     def side_of(c):
-        return int(c in (1, 2))
+        return c
 
     def multiply(c):
         landed(arrivals[c])
@@ -351,6 +356,7 @@
     hop(0, 1)
     group_start()
     hop(1, 1)
+    prepare(0)
     hop(0, 2)
     landed(need_in)
     copy = pltpu.make_async_copy(table, lookup, table_sem)
@@ -360,10 +366,12 @@
     hop(2, 1)
     hop(1, 2)
     hop(0, 3)
+    prepare(last)
     pick(0, near_part)
     spread(0, near_part)
     hop(2, 2)
     hop(1, 3)
+    prepare(1)
     hop(0, 4)
     group_hop(1)
     pick(0, far_part)
@@ -371,31 +379,28 @@
     spread(0, far_part)
     hop(2, 3)
     hop(1, 4)
+    prepare(2)
     pick(1, whole)
     forward(0, far_part)
     spread(1, whole)
     hop(2, 4)
     group_hop(2)
-    prepare(0)
     pick(2, whole)
     group_hop(3)
     multiply(0)
     forward(1, whole)
     spread(2, whole)
-    prepare(1)
-    prepare(last)
     group_hop(4)
     multiply(1)
     forward(2, whole)
     group_pick()
-    prepare(2)
     multiply(last)
+    sent()
     multiply(2)
     for copy in kept:
         copy.wait()
     landed(handed)
-    for copy in started:
-        copy.wait_send()
+    sent()
 
 
 def invert_kernel(counts_ref, stacked_ref, inner_ref, cos_ref, sin_ref, outer_ref, weight_ref, out_ref):
@@ -454,7 +459,7 @@
             pltpu.VMEM((NZ, NX, NY, 4, 16, 128), BF16),
             pltpu.VMEM((CHUNKS, 2 * NX, NZ, NY, 16, 128), BF16),
             pltpu.VMEM((RINGS, 2, NZ, NY, 16, 128), BF16),
-            pltpu.VMEM((2, 4, 2, 4, 8, 8, 128), F32),
+            pltpu.VMEM((CHUNKS, 4, 2, 4, 8, 8, 128), F32),
             pltpu.VMEM((CHUNKS, SLOTS, 32, 128), BF16),
             pltpu.VMEM((2 * NX, 8, 128), jnp.int32),
             pltpu.SMEM((2 * NX, 8, 128), jnp.int32),

time: 77.6 us -> 76.4 us (0.985)
  Pallas kernels: 74.7 us -> 73.9 us
    pallas_call x1, Pallas kernels: 71 us -> 70.2 us  [local(): pl.pallas_call(exchange_kernel, out_shape=jax.ShapeDtypeStruct((NY, CHUNK...]
where the time goes in v4:
time: 76.4 us; the launch traced here: 75.9 us
  Pallas kernels  73.9 us (97%)
  local copies, waits for them, and re-layouts  1.25 us (2%)
    pallas_call x1, Pallas kernels, local(): pl.pallas_call(exchange_kernel, out_shape=jax.ShapeDtypeStruct((NY, CHUNK...  70.2 us
    pallas_call x1, Pallas kernels, local(): pl.pallas_call(invert_kernel, out_shape=jax.ShapeDtypeStruct((8, 4, 128,...  3.67 us

profile of v4, /device:TPU:1, one launch (start us, length us, event | category | flops | bytes accessed | tf_op | source)
XLA Modules:
  0.0 75.9 jit_solution(49785615786778980)
XLA Ops:
  0.7 0.0 copy-start.1
  0.7 0.0 copy-start.2
  0.7 0.0 copy-start.3
  0.7 0.0 copy-start.4
  0.7 0.0 copy-start.5
  0.7 70.2 %exchange.1.stacked_ref = bf16[4,4,8,32,128]{4,3,2,1,0:T(8,128)(2,1)} custom-call(f32[1024,128]{1,0:T(8,128)} %bitcast.11, f32[512,256]{1,0:T(8,128)} %constant.18.clone.outer_ref, f32[256,128]{1,0:T(8,128)} %constant.19.clone.cos_ref, f32[256,128]{1,0:T(8,128)} %constant.20.clone.sin_ref, f32[256,128]{1,0:T(8,128)} %constant.21.clone.inner_ref, ...), custom_call_target="tpu_custom_call" | custom-call | tf_op jit(solution)/shard_map/exchange/pallas_call | solution.py:442
  70.9 0.0 copy-done.1
  70.9 0.0 copy-done.2
  70.9 0.0 copy-done.3
  71.0 0.0 copy-done.4
  71.0 0.0 copy-done.5
  71.0 0.0 copy-start
  71.0 1.2 %copy-done = bf16[4,4,8,32,128]{4,3,2,1,0:T(8,128)(2,1)S(1)} copy-done((bf16[4,4,8,32,128]{4,3,2,1,0:T(8,128)(2,1)S(1)}, bf16[4,4,8,32,128]{4,3,2,1,0:T(8,128)(2,1)}, u32[]{:S(2)}) %copy-start) | copy-done | bytes 1048600
  72.2 3.7 %invert.1 = bf16[8,4,128,128]{3,2,1,0:T(8,128)(2,1)} custom-call(s32[1]{0:T(128)S(6)} %copy.15.counts_ref, bf16[4,4,8,32,128]{4,3,2,1,0:T(8,128)(2,1)S(1)} %copy-done, bf16[256,256]{1,0:T(8,128)(2,1)S(1)} %copy-done.2, f32[16,8,128]{2,1,0:T(8,128)S(1)} %copy-done.4, f32[16,8,128]{2,1,0:T(8,128)S(1)} %copy-done.3, bf16[128,768]{1,0:T(8,128)(2,1)S(1)} %copy-done.1, ...), custom_call_target="tpu_custom_call" | custom-call | tf_op jit(solution)/shard_map/invert/pallas_call | solution.py:483
Async XLA Ops:
  0.7 70.3 %copy-start.1 = (bf16[128,768]{1,0:T(8,128)(2,1)S(1)}, bf16[128,768]{1,0:T(8,128)(2,1)}, u32[]{:S(2)}) copy-start(bf16[128,768]{1,0:T(8,128)(2,1)} %constant.25.clone.outer_ref) | copy-start | bytes 589828
  0.7 70.3 %copy-start.2 = (bf16[256,256]{1,0:T(8,128)(2,1)S(1)}, bf16[256,256]{1,0:T(8,128)(2,1)}, u32[]{:S(2)}) copy-start(bf16[256,256]{1,0:T(8,128)(2,1)} %constant.22.clone.inner_ref) | copy-start | bytes 393220
  0.7 70.3 %copy-start.3 = (f32[16,8,128]{2,1,0:T(8,128)S(1)}, f32[16,8,128]{2,1,0:T(8,128)}, u32[]{:S(2)}) copy-start(f32[16,8,128]{2,1,0:T(8,128)} %constant.24.clone.sin_ref) | copy-start | bytes 196612
  0.7 70.3 %copy-start.4 = (f32[16,8,128]{2,1,0:T(8,128)S(1)}, f32[16,8,128]{2,1,0:T(8,128)}, u32[]{:S(2)}) copy-start(f32[16,8,128]{2,1,0:T(8,128)} %constant.23.clone.cos_ref) | copy-start | bytes 196612
  0.7 70.3 %copy-start.5 = (bf16[32,128]{1,0:T(8,128)(2,1)S(1)}, bf16[32,128]{1,0:T(8,128)(2,1)}, u32[]{:S(2)}) copy-start(bf16[32,128]{1,0:T(8,128)(2,1)} %constant.26.clone.weight_ref) | copy-start | bytes 24580
  71.0 1.2 %copy-start = (bf16[4,4,8,32,128]{4,3,2,1,0:T(8,128)(2,1)S(1)}, bf16[4,4,8,32,128]{4,3,2,1,0:T(8,128)(2,1)}, u32[]{:S(2)}) copy-start(bf16[4,4,8,32,128]{4,3,2,1,0:T(8,128)(2,1)} %exchange.1.stacked_ref) | copy-start | bytes 3145732

commit v5 on v4

--- a/solution.py
+++ b/solution.py
@@ -385,8 +385,8 @@
     spread(1, whole)
     hop(2, 4)
     group_hop(2)
+    group_hop(3)
     pick(2, whole)
-    group_hop(3)
     multiply(0)
     forward(1, whole)
     spread(2, whole)

time: 76.4 us -> 76.4 us (level)
  no operation moved by 1% of the time
where the time goes in v5:
time: 76.4 us; the launch traced here: 75.9 us
  Pallas kernels  73.9 us (97%)
  local copies, waits for them, and re-layouts  1.25 us (2%)
    pallas_call x1, Pallas kernels, local(): pl.pallas_call(exchange_kernel, out_shape=jax.ShapeDtypeStruct((NY, CHUNK...  70.2 us
    pallas_call x1, Pallas kernels, local(): pl.pallas_call(invert_kernel, out_shape=jax.ShapeDtypeStruct((8, 4, 128,...  3.67 us

profile of v5, /device:TPU:1, one launch (start us, length us, event | category | flops | bytes accessed | tf_op | source)
XLA Modules:
  0.0 75.9 jit_solution(13720976252313916134)
XLA Ops:
  0.7 0.0 copy-start.1
  0.7 0.0 copy-start.2
  0.7 0.0 copy-start.3
  0.7 0.0 copy-start.4
  0.7 0.0 copy-start.5
  0.7 70.2 %exchange.1.stacked_ref = bf16[4,4,8,32,128]{4,3,2,1,0:T(8,128)(2,1)} custom-call(f32[1024,128]{1,0:T(8,128)} %bitcast.11, f32[512,256]{1,0:T(8,128)} %constant.18.clone.outer_ref, f32[256,128]{1,0:T(8,128)} %constant.19.clone.cos_ref, f32[256,128]{1,0:T(8,128)} %constant.20.clone.sin_ref, f32[256,128]{1,0:T(8,128)} %constant.21.clone.inner_ref, ...), custom_call_target="tpu_custom_call" | custom-call | tf_op jit(solution)/shard_map/exchange/pallas_call | solution.py:442
  70.9 0.0 copy-done.1
  70.9 0.0 copy-done.2
  70.9 0.0 copy-done.3
  71.0 0.0 copy-done.4
  71.0 0.0 copy-done.5
  71.0 0.0 copy-start
  71.0 1.2 %copy-done = bf16[4,4,8,32,128]{4,3,2,1,0:T(8,128)(2,1)S(1)} copy-done((bf16[4,4,8,32,128]{4,3,2,1,0:T(8,128)(2,1)S(1)}, bf16[4,4,8,32,128]{4,3,2,1,0:T(8,128)(2,1)}, u32[]{:S(2)}) %copy-start) | copy-done | bytes 1048600
  72.2 3.7 %invert.1 = bf16[8,4,128,128]{3,2,1,0:T(8,128)(2,1)} custom-call(s32[1]{0:T(128)S(6)} %copy.15.counts_ref, bf16[4,4,8,32,128]{4,3,2,1,0:T(8,128)(2,1)S(1)} %copy-done, bf16[256,256]{1,0:T(8,128)(2,1)S(1)} %copy-done.2, f32[16,8,128]{2,1,0:T(8,128)S(1)} %copy-done.4, f32[16,8,128]{2,1,0:T(8,128)S(1)} %copy-done.3, bf16[128,768]{1,0:T(8,128)(2,1)S(1)} %copy-done.1, ...), custom_call_target="tpu_custom_call" | custom-call | tf_op jit(solution)/shard_map/invert/pallas_call | solution.py:483
Async XLA Ops:
  0.7 70.3 %copy-start.1 = (bf16[128,768]{1,0:T(8,128)(2,1)S(1)}, bf16[128,768]{1,0:T(8,128)(2,1)}, u32[]{:S(2)}) copy-start(bf16[128,768]{1,0:T(8,128)(2,1)} %constant.25.clone.outer_ref) | copy-start | bytes 589828
  0.7 70.3 %copy-start.2 = (bf16[256,256]{1,0:T(8,128)(2,1)S(1)}, bf16[256,256]{1,0:T(8,128)(2,1)}, u32[]{:S(2)}) copy-start(bf16[256,256]{1,0:T(8,128)(2,1)} %constant.22.clone.inner_ref) | copy-start | bytes 393220
  0.7 70.3 %copy-start.3 = (f32[16,8,128]{2,1,0:T(8,128)S(1)}, f32[16,8,128]{2,1,0:T(8,128)}, u32[]{:S(2)}) copy-start(f32[16,8,128]{2,1,0:T(8,128)} %constant.24.clone.sin_ref) | copy-start | bytes 196612
  0.7 70.3 %copy-start.4 = (f32[16,8,128]{2,1,0:T(8,128)S(1)}, f32[16,8,128]{2,1,0:T(8,128)}, u32[]{:S(2)}) copy-start(f32[16,8,128]{2,1,0:T(8,128)} %constant.23.clone.cos_ref) | copy-start | bytes 196612
  0.7 70.3 %copy-start.5 = (bf16[32,128]{1,0:T(8,128)(2,1)S(1)}, bf16[32,128]{1,0:T(8,128)(2,1)}, u32[]{:S(2)}) copy-start(bf16[32,128]{1,0:T(8,128)(2,1)} %constant.26.clone.weight_ref) | copy-start | bytes 24580
  71.0 1.2 %copy-start = (bf16[4,4,8,32,128]{4,3,2,1,0:T(8,128)(2,1)S(1)}, bf16[4,4,8,32,128]{4,3,2,1,0:T(8,128)(2,1)}, u32[]{:S(2)}) copy-start(bf16[4,4,8,32,128]{4,3,2,1,0:T(8,128)(2,1)} %exchange.1.stacked_ref) | copy-start | bytes 3145732
